TPU v7x, 128 devices: a whole 4x4x4 slice. The times are simulated.
128 devices in a mesh: dp: 4 (over x), db: 32 (over z, y, core).
Axes of the slice: x: 4, y: 4, z: 4, core: 2. Of those that a mesh axis runs over, the one named last changes fastest.
Arguments:
- tokens: bfloat16 [2048, 64, 1024], P(('dp', 'db')), may hold values from -6 to 6
- neighbours: int32 [2048, 2], P(('dp', 'db')), may hold values from 0 to 2047, as said below
- database: bfloat16 [2048, 64, 1024], P('db'), may hold values from -256 to 256
- norm_gain: float32 [1024], replicated, may hold values from 0.1 to 1.9
- q_weight: bfloat16 [1024, 1024], P(('dp', 'db')), may hold values from -0.1875 to 0.1875
- key_weight: bfloat16 [1024, 1024], P(('dp', 'db')), may hold values from -0.1875 to 0.1875
- value_weight: bfloat16 [1024, 1024], P(('dp', 'db')), may hold values from -0.1875 to 0.1875
- out_weight: bfloat16 [1024, 1024], P(('dp', 'db')), may hold values from -0.1875 to 0.1875
Outputs:
- mixed: bfloat16 [2048, 64, 1024], P(('dp', 'db'))
Inputs may be any that keep to these rules, and one draw needn't show every extreme that they name: The two neighbours of a span are different database spans. Among the 32 neighbours of the spans of one device, at most 2 lie in one index of db's 64 spans; in every draw, for each index of dp, some index of db receives exactly 2 from every device of that dp index.
All inputs are finite; a program needn't handle non-finite values.
Results may differ from a plain program's by a relative error of at most 0.0035.
The roundings to bfloat16 on the way count: a program that leaves them out, or rounds other values in their place, can miss the bound.
Values may be sent and summed in bfloat16 or wider, within the bound.
No kernel may reach another device: no remote copies, remote signals or barrier semaphores. Data moves between devices by JAX's collectives and lax.ppermute only.
A program may use at most 128 MiB of HBM per device.

v0:
```python
import math

import jax
import jax.numpy as jnp
from jax import lax
from jax.sharding import PartitionSpec as P

HEADS = 16


def attend(queries, key_rows, value_rows, model_width):
    head_dim = queries.shape[-1]
    scores = jnp.einsum(
        "cihd,cnjhd->cnhij", queries, key_rows, preferred_element_type=jnp.float32
    ) / math.sqrt(head_dim)
    row_peak = jnp.max(scores, axis=-1, keepdims=True)
    exponent = jnp.exp(scores - row_peak)
    totals = jnp.sum(exponent, axis=-1)
    probs = exponent.astype(jnp.bfloat16)
    partial_value = jnp.einsum(
        "cnhij,cnjhd->cnhid", probs, value_rows, preferred_element_type=jnp.float32
    )
    peaks = row_peak[..., 0]
    best_peak = jnp.max(peaks, axis=1, keepdims=True)
    rescale = jnp.exp(peaks - best_peak)
    numerator = jnp.sum(rescale[..., None] * partial_value, axis=1)
    denominator = jnp.sum(rescale * totals, axis=1)
    attended = numerator / denominator[..., None]
    joined = jnp.transpose(attended, (0, 2, 1, 3))
    return joined.reshape(joined.shape[0], joined.shape[1], model_width).astype(jnp.bfloat16)


def shards(tokens, neighbours, database, norm_gain, q_weight, key_weight, value_weight, out_weight):
    w_query, w_key, w_value, w_out = (
        lax.all_gather(q_weight, ("dp", "db"), axis=0, tiled=True),
        lax.all_gather(key_weight, ("dp", "db"), axis=0, tiled=True),
        lax.all_gather(value_weight, ("dp", "db"), axis=0, tiled=True),
        lax.all_gather(out_weight, ("dp", "db"), axis=0, tiled=True),
    )
    spans, length, model_width = tokens.shape
    head_dim = model_width // HEADS
    holders = lax.axis_size("db")
    slab_size = database.shape[0]
    wanted_ids = neighbours.reshape(-1)
    needed = wanted_ids.shape[0]
    capacity = 2 * needed // holders
    slots_n = holders * capacity
    holder_of = wanted_ids // slab_size
    local_row = wanted_ids % slab_size
    positions = jnp.arange(needed, dtype=jnp.int32)
    earlier = (holder_of[None, :] == holder_of[:, None]) & (positions[None, :] < positions[:, None])
    rank_of = jnp.sum(earlier.astype(jnp.int32), axis=1)
    slot_of = holder_of * capacity + rank_of
    onehot = (slot_of[:, None] == jnp.arange(slots_n, dtype=jnp.int32)[None, :]).astype(jnp.int32)
    wanted = (jnp.sum(onehot * (local_row + 1)[:, None], axis=0) - 1).reshape(holders, capacity)
    incoming = lax.all_to_all(wanted, "db", split_axis=0, concat_axis=0, tiled=True)
    filled = incoming >= 0
    slab_rows = jnp.maximum(incoming, 0).reshape(-1)
    picked = jnp.where(
        filled.reshape(-1)[:, None, None], database[slab_rows], jnp.zeros((), jnp.bfloat16)
    )
    picked = picked.reshape(holders, capacity, length, model_width)
    blocks = lax.all_to_all(picked, "db", split_axis=0, concat_axis=0, tiled=True)
    flattened = blocks.reshape(-1, model_width)
    key_part = jnp.dot(flattened, w_key, preferred_element_type=jnp.float32).astype(jnp.bfloat16)
    value_part = jnp.dot(flattened, w_value, preferred_element_type=jnp.float32).astype(
        jnp.bfloat16
    )
    keys_all = key_part.reshape(blocks.shape)
    values_all = value_part.reshape(blocks.shape)
    key_rows = keys_all.reshape(slots_n, length, model_width)[slot_of]
    value_rows = values_all.reshape(slots_n, length, model_width)[slot_of]
    key_rows = key_rows.reshape(spans, 2, length, HEADS, head_dim)
    value_rows = value_rows.reshape(spans, 2, length, HEADS, head_dim)
    floated = tokens.astype(jnp.float32)
    normed = (
        floated * lax.rsqrt(jnp.mean(floated * floated, axis=-1, keepdims=True) + 1e-05) * norm_gain
    ).astype(jnp.bfloat16)
    queries = jnp.dot(
        normed.reshape(-1, model_width), w_query, preferred_element_type=jnp.float32
    ).astype(jnp.bfloat16)
    queries = queries.reshape(spans, length, HEADS, head_dim)
    attended = attend(queries, key_rows, value_rows, model_width)
    projected = jnp.dot(
        attended.reshape(-1, model_width), w_out, preferred_element_type=jnp.float32
    )
    return (floated + projected.reshape(spans, length, model_width)).astype(jnp.bfloat16)


def solution(mesh):
    placed = (
        P(("dp", "db"), None, None),
        P(("dp", "db"), None),
        P("db", None, None),
        P(),
        P(("dp", "db"), None),
        P(("dp", "db"), None),
        P(("dp", "db"), None),
        P(("dp", "db"), None),
    )
    return jax.shard_map(
        shards, mesh=mesh, in_specs=placed, out_specs=P(("dp", "db"), None, None), check_vma=False
    )
```

profile of v0, /device:TPU:113, one launch (start us, length us, event | category | flops | bytes accessed | tf_op | source)
XLA Modules:
  0.0 346.9 jit_solution(17183272506412114574)
XLA Ops:
  6.5 0.7 all-gather.7.cloned.1.call-update
  7.3 0.7 all-gather.5.cloned.1.call-update
  8.0 0.8 copy.46
  8.9 0.2 convert_reduce_fusion
  9.3 10.6 %all_to_all.11 = s32[32,1,2]{2,1,0:T(1,128)S(1)} all-to-all(s32[32,1,2]{2,1,0:T(1,128)S(1)} %bitcast.49), channel_id=1, replica_groups=mesh['dp'=4,'db'=32] {'db'}, dimensions={0} | all-to-all | bytes 512 | tf_op jit(solution)/shard_map/all_to_all | solution.py:56
  20.3 8.8 %gather_fusion = bf16[64,64,1024]{2,1,0:T(8,128)(2,1)} fusion(bf16[64,64,1024]{2,1,0:T(8,128)(2,1)} %param.10, s32[1024]{0:T(1024)S(1)} %pad_clamp_fusion.1), kind=kCustom, calls=%fused_computation | custom fusion | bytes 16777472 | tf_op jit(solution)/shard_map/gather | solution.py:60
  29.1 7.2 %broadcast_select_fusion = bf16[32,2,64,1024]{3,2,1,0:T(8,128)(2,1)} fusion(bf16[32,2,64,1024]{3,2,1,0:T(8,128)(2,1)} %bitcast.44, pred[32,2]{1,0:T(8,128)(4,1)S(1)} %copy.49), kind=kLoop, calls=%fused_computation.17 | loop fusion | flops 4194304 | bytes 16777280 | tf_op jit(solution)/shard_map/jit(_where)/select_n | solution.py:59
  36.3 8.9 %all-to-all-start.1 = ((bf16[32,2,64,1024]{3,2,1,0:T(8,128)(2,1)}), bf16[32,2,64,1024]{3,2,1,0:T(8,128)(2,1)}, u32[]{:S(2)}, u32[]{:S(2)}) async-start(bf16[32,2,64,1024]{3,2,1,0:T(8,128)(2,1)} %broadcast_select_fusion), calls=%async_computation.1 | async-start | bytes 16777216 | tf_op jit(solution)/shard_map/all_to_all | solution.py:63
  45.3 0.7 all-gather.9.cloned.1.call-update
  46.1 0.5 all-gather.11.cloned.1.call-update
  46.7 0.5 fusion.9
  47.2 1.9 fusion.11
  49.1 62.5 %all-gather.7.cloned.1.call-done = bf16[1024,1024]{1,0:T(8,128)(2,1)} async-done(((bf16[8,1024]{1,0:T(8,128)(2,1)}), bf16[1024,1024]{1,0:T(8,128)(2,1)}) %all-gather.7.cloned.1.call-update) | async-done | bytes 2097168 | tf_op jit(solution)/shard_map/all_gather | solution.py:35
  111.5 5.9 %convolution_convert_fusion.2 = bf16[1024,1024]{1,0:T(8,128)(2,1)} fusion(bf16[1024,1024]{1,0:T(8,128)(2,1)} %bitcast.45, bf16[1024,1024]{1,0:T(8,128)(2,1)} %all-gather.7.cloned.1.call-done), kind=kOutput, calls=%fused_computation.30 | convolution fusion | flops 2148532224 | bytes 6291456 | tf_op jit(solution)/shard_map/dot_general | solution.py:79
  117.4 6.4 %reshape.248 = bf16[16,64,16,64]{3,2,1,0:T(8,128)(2,1)} reshape(bf16[1024,1024]{1,0:T(8,128)(2,1)} %convolution_convert_fusion.2) | data formatting | bytes 4194304 | tf_op jit(solution)/shard_map/reshape | solution.py:82
  123.9 78.6 %all-gather.5.cloned.1.call-done = bf16[1024,1024]{1,0:T(8,128)(2,1)} async-done(((bf16[8,1024]{1,0:T(8,128)(2,1)}), bf16[1024,1024]{1,0:T(8,128)(2,1)}) %all-gather.5.cloned.1.call-update) | async-done | bytes 2097168 | tf_op jit(solution)/shard_map/all_gather | solution.py:36
  202.5 14.9 %convolution_convert_fusion.1 = bf16[4096,1024]{1,0:T(8,128)(2,1)} fusion(bf16[4096,1024]{1,0:T(8,128)(2,1)} %bitcast.3, bf16[1024,1024]{1,0:T(8,128)(2,1)} %all-gather.5.cloned.1.call-done), kind=kOutput, calls=%fused_computation.19 | convolution fusion | flops 8594128896 | bytes 18874368 | tf_op jit(solution)/shard_map/dot_general | solution.py:65
  217.4 6.2 %gather_fusion.1 = bf16[32,64,1024]{2,1,0:T(8,128)(2,1)} fusion(bf16[64,64,1024]{2,1,0:T(8,128)(2,1)} %bitcast.47, s32[1024]{0:T(1024)S(1)} %pad_clamp_fusion), kind=kCustom, calls=%fused_computation.1 | custom fusion | bytes 8388736 | tf_op jit(solution)/shard_map/gather | solution.py:71
  223.6 11.6 %reshape.246 = bf16[16,2,64,16,64]{4,3,2,1,0:T(8,128)(2,1)} reshape(bf16[32,64,1024]{2,1,0:T(8,128)(2,1)} %gather_fusion.1) | data formatting | bytes 8388608 | tf_op jit(solution)/shard_map/reshape | solution.py:73
  235.2 11.7 %bitcast_reduce_fusion.1 = (f32[16,2,16,64]{3,1,2,0:T(2,128)S(1)}, f32[16,16,2,64,64]{4,3,2,1,0:T(8,128)}) fusion(bf16[16,64,16,64,1]{3,2,1,0,4:T(8,128)(2,1)} %bitcast.43, bf16[16,2,64,16,64]{4,3,2,1,0:T(8,128)(2,1)} %reshape.246), kind=kOutput, calls=%fused_computation.5 | convolution fusion | flops 272596992 | bytes 14811136 | tf_op jit(solution)/shard_map/cihd,cnjhd->cnhij/dot_general | solution.py:13
  246.9 12.7 %fusion.1 = (f32[16,2,16,64]{3,1,2,0:T(2,128)S(1)}, f32[16,16,64]{2,1,0:T(8,128)S(1)}, bf16[16,2,16,64,64]{3,4,1,2,0:T(8,128)(2,1)}) fusion(f32[16,16,2,64,64]{4,3,2,1,0:T(8,128)} %get-tuple-element.13, f32[16,2,16,64]{3,1,2,0:T(2,128)S(1)} %get-tuple-element.12), kind=kLoop, calls=%fused_computation.8 | loop fusion | flops 10436608 | bytes 12910592 | tf_op jit(solution)/shard_map/reduce_sum | solution.py:18
  259.6 0.5 multiply_reduce_fusion.1
  260.1 8.4 %all-gather.9.cloned.1.call-done = bf16[1024,1024]{1,0:T(8,128)(2,1)} async-done(((bf16[8,1024]{1,0:T(8,128)(2,1)}), bf16[1024,1024]{1,0:T(8,128)(2,1)}) %all-gather.9.cloned.1.call-update) | async-done | bytes 2097168 | tf_op jit(solution)/shard_map/all_gather | solution.py:37
  268.6 14.9 %convolution_convert_fusion = bf16[4096,1024]{1,0:T(8,128)(2,1)} fusion(bf16[4096,1024]{1,0:T(8,128)(2,1)} %bitcast.3, bf16[1024,1024]{1,0:T(8,128)(2,1)} %all-gather.9.cloned.1.call-done), kind=kOutput, calls=%fused_computation.18 | convolution fusion | flops 8594128896 | bytes 18874368 | tf_op jit(solution)/shard_map/dot_general | solution.py:66
  283.4 6.2 %gather_fusion.2 = bf16[32,64,1024]{2,1,0:T(8,128)(2,1)} fusion(bf16[64,64,1024]{2,1,0:T(8,128)(2,1)} %bitcast.46, s32[1024]{0:T(1024)S(1)} %pad_clamp_fusion), kind=kCustom, calls=%fused_computation.2 | custom fusion | bytes 8388736 | tf_op jit(solution)/shard_map/gather | solution.py:72
  289.6 11.6 %reshape.249 = bf16[16,2,64,16,64]{4,3,2,1,0:T(8,128)(2,1)} reshape(bf16[32,64,1024]{2,1,0:T(8,128)(2,1)} %gather_fusion.2) | data formatting | bytes 8388608 | tf_op jit(solution)/shard_map/reshape | solution.py:74
  301.2 11.2 %multiply_reduce_fusion = f32[16,16,64,64]{3,2,1,0:T(8,128)S(1)} fusion(f32[16,2,16,64]{3,2,1,0:T(8,128)S(1)} %copy.53, bf16[16,2,64,16,64]{4,3,2,1,0:T(8,128)(2,1)} %reshape.249, bf16[16,2,16,64,64]{3,4,1,2,0:T(8,128)(2,1)} %get-tuple-element.9), kind=kOutput, calls=%fused_computation.7 | convolution fusion | flops 271581184 | bytes 12713984 | tf_op jit(solution)/shard_map/cnhij,cnjhd->cnhid/dot_general | solution.py:20
  312.4 2.8 fusion.3
  315.2 5.5 %copy.56 = bf16[16,64,16,64]{3,2,1,0:T(8,128)(2,1)} copy(bf16[16,64,16,64]{3,1,2,0:T(8,128)(2,1)S(1)} %fusion.3) | data formatting | bytes 4194304 | tf_op jit(solution)/shard_map/convert_element_type | solution.py:30
  320.7 6.6 %convert_element_type.41 = bf16[16,64,1024]{2,1,0:T(8,128)(2,1)} reshape(bf16[16,64,16,64]{3,2,1,0:T(8,128)(2,1)} %copy.56) | data formatting | bytes 4194304 | tf_op jit(solution)/shard_map/convert_element_type | solution.py:30
  327.3 7.2 %all-gather.11.cloned.1.call-done = bf16[1024,1024]{1,0:T(8,128)(2,1)} async-done(((bf16[8,1024]{1,0:T(8,128)(2,1)}), bf16[1024,1024]{1,0:T(8,128)(2,1)}) %all-gather.11.cloned.1.call-update) | async-done | bytes 2097168 | tf_op jit(solution)/shard_map/all_gather | solution.py:38
  334.5 5.9 %fusion.12 = bf16[16,64,1024]{2,1,0:T(8,128)(2,1)} fusion(bf16[16,64,1024]{2,1,0:T(8,128)(2,1)S(1)} %copy-done, bf16[16,64,1024]{2,1,0:T(8,128)(2,1)} %convert_element_type.41, bf16[1024,1024]{1,0:T(8,128)(2,1)} %all-gather.11.cloned.1.call-done), kind=kOutput, calls=%fused_computation.26 | convolution fusion | flops 2150629376 | bytes 8388608 | tf_op jit(solution)/shard_map/dot_general | solution.py:84
  (26 shorter events, 0.9 us)
Async XLA Ops:
  6.5 105.0 %all-gather.7.cloned.1.call-start = ((), (), s32[]{:S(2)}) async-start(), calls=%async_computation.3 | async-start | bytes 2113536 | tf_op jit(solution)/shard_map/all_gather | solution.py:35
  7.3 195.2 %all-gather.5.cloned.1.call-start = ((), (), s32[]{:S(2)}) async-start(), calls=%async_computation.2 | async-start | bytes 2113536 | tf_op jit(solution)/shard_map/all_gather | solution.py:36
  36.3 10.4 %copy-start = (bf16[16,64,1024]{2,1,0:T(8,128)(2,1)S(1)}, bf16[16,64,1024]{2,1,0:T(8,128)(2,1)}, u32[]{:S(2)}) copy-start(bf16[16,64,1024]{2,1,0:T(8,128)(2,1)} %param.8) | copy-start | bytes 6291460
  36.3 10.9 %copy-start.1 = (f32[1024]{0:T(1024)S(1)}, f32[1024]{0:T(1024)}, u32[]{:S(2)}) copy-start(f32[1024]{0:T(1024)} %param.11) | copy-start | bytes 12292
  36.3 166.2 %all-to-all-start.1 = ((bf16[32,2,64,1024]{3,2,1,0:T(8,128)(2,1)}), bf16[32,2,64,1024]{3,2,1,0:T(8,128)(2,1)}, u32[]{:S(2)}, u32[]{:S(2)}) async-start(bf16[32,2,64,1024]{3,2,1,0:T(8,128)(2,1)} %broadcast_select_fusion), calls=%async_computation.1 | async-start | bytes 16777216 | tf_op jit(solution)/shard_map/all_to_all | solution.py:63
  45.3 223.3 %all-gather.9.cloned.1.call-start = ((), (), s32[]{:S(2)}) async-start(), calls=%async_computation.4 | async-start | bytes 2113536 | tf_op jit(solution)/shard_map/all_gather | solution.py:37
  46.0 288.5 %all-gather.11.cloned.1.call-start = ((), (), s32[]{:S(2)}) async-start(), calls=%async_computation.5 | async-start | bytes 2113536 | tf_op jit(solution)/shard_map/all_gather | solution.py:38
Sparse Core Ops, SparseCore 0:
  10.5 100.9 all-gather.6
  114.7 87.7 all-gather.4
  205.7 62.8 all-gather.8
  271.6 62.8 all-gather.10
where the time goes:
time: 353 us; the launch traced here: 347 us
  waiting for transfers between devices  159 us (45%)
  matrix products  64.5 us (18%)
  local copies, waits for them, and re-layouts  64.2 us (18%)
  other arithmetic  26 us (7%)
  between operations  13.3 us (4%)
  blocking collectives  10.6 us (3%)
  starting transfers between devices  9.05 us (3%)
    all_gather x1, waiting for transfers between devices, shards(): lax.all_gather(key_weight, ('dp', 'db'), axis=0, tiled=True)  78.6 us
    all_gather x1, waiting for transfers between devices, shards(): lax.all_gather(q_weight, ('dp', 'db'), axis=0, tiled=True)  62.5 us
    dot_general x1, matrix products, shards(): jnp.dot(flattened, w_key, preferred_element_type=jnp.float32)  14.9 us
    dot_general x1, matrix products, shards(): jnp.dot(flattened, w_value, preferred_element_type=jnp.float32)  14.9 us
    reduce_sum x1, other arithmetic, attend(): totals = jnp.sum(exponent, axis=-1)  12.7 us
    convert_element_type x2, local copies, waits for them, and re-layouts, attend(): joined.reshape(joined.shape[0], joined.shape[1], model_width)  12.1 us
    dot_general x1, matrix products, attend(): jnp.einsum('cihd,cnjhd->cnhij', queries, key_rows, preferred_element_type...  11.7 us
    reshape x1, local copies, waits for them, and re-layouts, shards(): key_rows = key_rows.reshape(spans, 2, length, HEADS, head_dim)  11.6 us
  transfers between devices with their start and end apart: 5, of which 4 were waited for; matrix products, arithmetic and copies ran while one was open for 43% of the time, Pallas kernels for 0%

commit v1 on v0

v1 whole, which is shorter than its diff:
```python
import functools

import jax
import jax.numpy as jnp
from jax import lax
from jax.experimental import pallas as pl
from jax.experimental.pallas import tpu as pltpu
from jax.sharding import PartitionSpec as P

HEADS = 16
GROUP = 4
ANY = pl.ANY


def gather_kernel(rows_ref, table_ref, out_ref, held, in_sems, out_sems):
    count = held.shape[0]

    def read(i):
        return pltpu.make_async_copy(table_ref.at[rows_ref[i]], held.at[i], in_sems.at[i])

    def write(i):
        return pltpu.make_async_copy(held.at[i], out_ref.at[i], out_sems.at[i])

    for i in range(count):
        read(i).start()
    for i in range(count):
        read(i).wait()
        write(i).start()
    for i in range(count):
        write(i).wait()


def gather_rows(table, rows):
    count = rows.shape[0]
    shape = (count,) + table.shape[1:]
    nbytes = 2 * count * table.shape[1] * table.shape[2]
    return pl.pallas_call(
        gather_kernel,
        out_shape=jax.ShapeDtypeStruct(shape, table.dtype),
        grid_spec=pltpu.PrefetchScalarGridSpec(
            num_scalar_prefetch=1,
            grid=(1,),
            in_specs=[pl.BlockSpec(memory_space=ANY)],
            out_specs=pl.BlockSpec(memory_space=ANY),
            scratch_shapes=[
                pltpu.VMEM(shape, table.dtype),
                pltpu.SemaphoreType.DMA((count,)),
                pltpu.SemaphoreType.DMA((count,)),
            ],
        ),
        cost_estimate=pl.CostEstimate(flops=0, bytes_accessed=2 * nbytes, transcendentals=0),
    )(rows, table)


def query_kernel(tokens_ref, gain_ref, w_ref, out_ref):
    floated = tokens_ref[...].astype(jnp.float32)
    mean = jnp.mean(floated * floated, axis=-1, keepdims=True)
    normed = (floated * lax.rsqrt(mean + 1e-05) * gain_ref[...]).astype(jnp.bfloat16)
    out_ref[...] = jnp.dot(normed, w_ref[...], preferred_element_type=jnp.float32).astype(
        jnp.bfloat16
    )


def project_queries(flat, gain, weights, tile=256):
    rows, width = flat.shape
    return pl.pallas_call(
        query_kernel,
        out_shape=jax.ShapeDtypeStruct((rows, width), jnp.bfloat16),
        grid=(rows // tile,),
        in_specs=[
            pl.BlockSpec((tile, width), lambda i: (i, 0)),
            pl.BlockSpec((1, width), lambda i: (0, 0)),
            pl.BlockSpec((width, width), lambda i: (0, 0)),
        ],
        out_specs=pl.BlockSpec((tile, width), lambda i: (i, 0)),
        cost_estimate=pl.CostEstimate(
            flops=2 * rows * width * width, bytes_accessed=6 << 20, transcendentals=0
        ),
    )(flat, gain, weights)


def keys_kernel(blocks_ref, w_key_ref, w_value_ref, out_ref):
    width = blocks_ref.shape[1]
    blocks = blocks_ref[...]
    out_ref[:, :width] = jnp.dot(
        blocks, w_key_ref[...], preferred_element_type=jnp.float32
    ).astype(jnp.bfloat16)
    out_ref[:, width:] = jnp.dot(
        blocks, w_value_ref[...], preferred_element_type=jnp.float32
    ).astype(jnp.bfloat16)


def project_blocks(flat, weights, tile=256):
    rows, width = flat.shape
    return pl.pallas_call(
        keys_kernel,
        out_shape=jax.ShapeDtypeStruct((rows, 2 * width), jnp.bfloat16),
        grid=(rows // tile,),
        in_specs=[
            pl.BlockSpec((tile, width), lambda i: (i, 0)),
            pl.BlockSpec((width, width), lambda i: (0, 1)),
            pl.BlockSpec((width, width), lambda i: (0, 2)),
        ],
        out_specs=pl.BlockSpec((tile, 2 * width), lambda i: (i, 0)),
        cost_estimate=pl.CostEstimate(
            flops=4 * rows * width * width, bytes_accessed=16 << 20, transcendentals=0
        ),
    )(flat, weights, weights)


def tail_kernel(
    holders,
    extra,
    length,
    meta_ref,
    tokens_ref,
    queries_ref,
    w_key_ref,
    w_value_ref,
    w_out_ref,
    first_ref,
    second_ref,
    out_ref,
    rows_held,
    blocks_held,
    joined,
    rows_sem,
    block_sems,
):
    step = pl.program_id(0)
    width = tokens_ref.shape[1]
    spans = tokens_ref.shape[0] // length
    lanes_n = GROUP * (width // HEADS)
    n_second = meta_ref[2 * holders]

    @pl.when(step == 0)
    def _():
        first = pltpu.make_async_copy(first_ref, rows_held.at[pl.ds(0, holders)], rows_sem)

        def read(i):
            return pltpu.make_async_copy(
                second_ref.at[meta_ref[holders + i]],
                blocks_held.at[pl.ds(i * length, length)],
                block_sems.at[i],
            )

        for i in range(extra):
            read(i).start()
        first.start()
        for i in range(extra):
            read(i).wait()
        for t in range(extra // 4):

            @pl.when(n_second > 4 * t)
            def _():
                blocks = blocks_held[4 * t * length : 4 * (t + 1) * length, :]
                for at, w_ref in ((0, w_key_ref), (width, w_value_ref)):
                    rows = jnp.dot(
                        blocks, w_ref[...], preferred_element_type=jnp.float32
                    ).astype(jnp.bfloat16)
                    rows_held[holders + 4 * t : holders + 4 * t + 4, :, at : at + width] = (
                        rows.reshape(4, length, width)
                    )

        first.wait()

    lane = lax.broadcasted_iota(jnp.int32, (1, lanes_n), 1) // (width // HEADS)

    def span(c, _):
        at = (step * spans + c) * 2
        one, two = meta_ref[at], meta_ref[at + 1]
        row = pl.multiple_of(c * length, length)
        for g in range(HEADS // GROUP):
            cols = slice(g * lanes_n, (g + 1) * lanes_n)
            vcols = slice(width + g * lanes_n, width + (g + 1) * lanes_n)
            queries = queries_ref[pl.ds(row, length), cols].astype(jnp.float32)
            stacked = jnp.concatenate(
                [jnp.where(lane == h, queries, 0.0) for h in range(GROUP)], axis=0
            ).astype(jnp.bfloat16)
            keys = jnp.concatenate([rows_held[one, :, cols], rows_held[two, :, cols]], axis=0)
            values = jnp.concatenate(
                [rows_held[one, :, vcols], rows_held[two, :, vcols]], axis=0
            )
            scores = lax.dot_general(
                stacked, keys, (((1,), (1,)), ((), ())), preferred_element_type=jnp.float32
            ) * ((width // HEADS) ** -0.5)
            peak = jnp.max(scores, axis=-1, keepdims=True)
            exponent = jnp.exp(scores - peak)
            totals = jnp.sum(exponent, axis=-1, keepdims=True)
            summed = jnp.dot(
                exponent.astype(jnp.bfloat16), values, preferred_element_type=jnp.float32
            ) / totals
            attended = summed[:length]
            for h in range(1, GROUP):
                attended = jnp.where(
                    lane == h, summed[h * length : (h + 1) * length], attended
                )
            joined[pl.ds(row, length), cols] = attended.astype(jnp.bfloat16)
        return _

    lax.fori_loop(0, spans, span, 0)
    projected = jnp.dot(joined[...], w_out_ref[...], preferred_element_type=jnp.float32)
    out_ref[...] = (tokens_ref[...].astype(jnp.float32) + projected).astype(jnp.bfloat16)


def finish(meta, flat, queries, weights, first, second, holders, extra, length, spans=4):
    rows, width = flat.shape
    tile = spans * length
    resident = pl.Buffered(1)
    return pl.pallas_call(
        functools.partial(tail_kernel, holders, extra, length),
        out_shape=jax.ShapeDtypeStruct((rows, width), jnp.bfloat16),
        grid_spec=pltpu.PrefetchScalarGridSpec(
            num_scalar_prefetch=1,
            grid=(rows // tile,),
            in_specs=[
                pl.BlockSpec((tile, width), lambda i, m: (i, 0)),
                pl.BlockSpec((tile, width), lambda i, m: (i, 0)),
                pl.BlockSpec((width, width), lambda i, m: (0, 1), pipeline_mode=resident),
                pl.BlockSpec((width, width), lambda i, m: (0, 2), pipeline_mode=resident),
                pl.BlockSpec((width, width), lambda i, m: (0, 3), pipeline_mode=resident),
                pl.BlockSpec(memory_space=ANY),
                pl.BlockSpec(memory_space=ANY),
            ],
            out_specs=pl.BlockSpec((tile, width), lambda i, m: (i, 0)),
            scratch_shapes=[
                pltpu.VMEM((holders + extra, length, 2 * width), jnp.bfloat16),
                pltpu.VMEM((extra * length, width), jnp.bfloat16),
                pltpu.VMEM((tile, width), jnp.bfloat16),
                pltpu.SemaphoreType.DMA,
                pltpu.SemaphoreType.DMA((extra,)),
            ],
        ),
        compiler_params=pltpu.CompilerParams(vmem_limit_bytes=48 << 20),
        cost_estimate=pl.CostEstimate(
            flops=15 << 30, bytes_accessed=24 << 20, transcendentals=2 << 20
        ),
    )(meta, flat, queries, weights, weights, weights, first, second)


def shards(tokens, neighbours, database, norm_gain, q_weight, key_weight, value_weight, out_weight):
    spans, length, width = tokens.shape
    holders = lax.axis_size("db")
    slab = database.shape[0]
    shard = jnp.concatenate([q_weight, key_weight, value_weight, out_weight], axis=1)
    weights = lax.all_gather(shard, ("dp", "db"), axis=0, tiled=True)

    wanted_ids = neighbours.reshape(-1)
    needed = wanted_ids.shape[0]
    extra = needed // 2
    holder_of = wanted_ids // slab
    local_row = wanted_ids % slab
    position = jnp.arange(needed, dtype=jnp.int32)
    earlier = position[None, :] < position[:, None]
    same = holder_of[None, :] == holder_of[:, None]
    rank_of = jnp.sum((same & earlier).astype(jnp.int32), axis=1)
    slot_of = rank_of * holders + holder_of
    hit = slot_of[:, None] == jnp.arange(2 * holders, dtype=jnp.int32)[None, :]
    wanted = jnp.sum(jnp.where(hit, local_row[:, None], 0), axis=0).reshape(2, holders)
    incoming = lax.all_to_all(wanted, "db", split_axis=1, concat_axis=1, tiled=True)
    rows = jnp.clip(incoming, 0, slab - 1)
    first = lax.all_to_all(
        gather_rows(database, rows[0]), "db", split_axis=0, concat_axis=0, tiled=True
    )
    second = lax.all_to_all(
        gather_rows(database, rows[1]), "db", split_axis=0, concat_axis=0, tiled=True
    )

    extra_of = jnp.sum(jnp.where(earlier, rank_of[None, :], 0), axis=1)
    place = jnp.where(rank_of == 0, holder_of, holders + extra_of)
    chosen = (rank_of[:, None] == 1) & (
        extra_of[:, None] == jnp.arange(extra, dtype=jnp.int32)[None, :]
    )
    extras = jnp.sum(jnp.where(chosen, holder_of[:, None], 0), axis=0)
    meta = jnp.concatenate(
        [place, extras, jnp.zeros((holders - extra,), jnp.int32), jnp.sum(rank_of)[None]]
    )

    flat = tokens.reshape(-1, width)
    queries = project_queries(flat, norm_gain.reshape(1, -1), weights)
    first_rows = project_blocks(first.reshape(-1, width), weights)
    mixed = finish(
        meta,
        flat,
        queries,
        weights,
        first_rows.reshape(holders, length, 2 * width),
        second,
        holders,
        extra,
        length,
    )
    return mixed.reshape(tokens.shape)


def solution(mesh):
    both = P(("dp", "db"), None)
    placed = (
        P(("dp", "db"), None, None),
        both,
        P("db", None, None),
        P(),
        both,
        both,
        both,
        both,
    )
    return jax.shard_map(
        shards, mesh=mesh, in_specs=placed, out_specs=P(("dp", "db"), None, None), check_vma=False
    )
```

time: 353 us -> 208 us (0.59); the launches traced: 347 us -> 207 us
  matrix products: 64.5 us -> 0 us
  waiting for transfers between devices: 159 us -> 95.3 us
  Pallas kernels: 0 us -> 60.9 us
  local copies, waits for them, and re-layouts: 64.2 us -> 4.49 us
  other arithmetic: 26 us -> 3.19 us
  starting transfers between devices: 9.05 us -> 19.5 us
    all_gather x4 -> x1, waiting for transfers between devices: 157 us -> 52.7 us  [shards(): weights = lax.all_gather(shard, ('dp', 'db'), axis=0, tiled=True)]
    dot_general x6 -> x0, matrix products: 64.5 us -> none  [the longest x1 14.9 us: shards(): jnp.dot(flattened, w_key, preferred_element_type=jnp.float32)]
    pallas_call x0 -> x5, Pallas kernels: none -> 60.9 us  [the longest x1 26.9 us: finish(): pl.pallas_call(functools.partial(tail_kernel, holders, extra, length), ou...]
    all_to_all x1 -> x2, waiting for transfers between devices: 0.01 us -> 42.6 us  [the longest x1 42.6 us: shards(): lax.all_to_all(gather_rows(database, rows[0]), 'db', split_axis=0, concat...]
    reshape x3 -> x0, local copies, waits for them, and re-layouts: 29.6 us -> none  [the longest x1 11.6 us: shards(): key_rows = key_rows.reshape(spans, 2, length, HEADS, head_dim)]
    gather x3 -> x0, local copies, waits for them, and re-layouts: 21.2 us -> none  [the longest x1 8.81 us: shards(): database[slab_rows]]
    reduce_sum x5 -> x4, other arithmetic: 14 us -> 1.06 us  [the longest x1 0.74 us: shards(): rank_of = jnp.sum((same & earlier).astype(jnp.int32), axis=1)]
    convert_element_type x2 -> x0, local copies, waits for them, and re-layouts: 12.1 us -> none  [attend(): joined.reshape(joined.shape[0], joined.shape[1], model_width)]
  transfers between devices with their start and end apart: 5 -> 3, of which waited for: 4 -> 2; matrix products, arithmetic and copies ran while one was open for 43% -> 2% of each run, Pallas kernels for 0% -> 16%
where the time goes in v1:
time: 208 us; the launch traced here: 207 us
  waiting for transfers between devices  95.3 us (46%)
  Pallas kernels  60.9 us (29%)
  starting transfers between devices  19.5 us (9%)
  between operations  13.5 us (6%)
  blocking collectives  10.6 us (5%)
  local copies, waits for them, and re-layouts  4.49 us (2%)
  other arithmetic  3.19 us (2%)
    all_gather x1, waiting for transfers between devices, shards(): weights = lax.all_gather(shard, ('dp', 'db'), axis=0, tiled=True)  52.7 us
    all_to_all x1, waiting for transfers between devices, shards(): lax.all_to_all(gather_rows(database, rows[0]), 'db', split_axis=0, concat...  42.6 us
    pallas_call x1, Pallas kernels, finish(): pl.pallas_call(functools.partial(tail_kernel, holders, extra, length), ou...  26.9 us
    pallas_call x1, Pallas kernels, project_blocks(): pl.pallas_call(keys_kernel, out_shape=jax.ShapeDtypeStruct((rows, 2 * wid...  14.2 us
    pallas_call x2, Pallas kernels, gather_rows(): pl.pallas_call(gather_kernel, out_shape=jax.ShapeDtypeStruct(shape, table...  13.5 us
    all_to_all x1, blocking collectives, shards(): lax.all_to_all(wanted, 'db', split_axis=1, concat_axis=1, tiled=True)  10.6 us
    all_to_all x1, starting transfers between devices, shards(): lax.all_to_all(gather_rows(database, rows[1]), 'db', split_axis=0, concat...  10.5 us
    all_to_all x1, starting transfers between devices, shards(): lax.all_to_all(gather_rows(database, rows[0]), 'db', split_axis=0, concat...  8.92 us
  transfers between devices with their start and end apart: 3, of which 2 were waited for; matrix products, arithmetic and copies ran while one was open for 2% of the time, Pallas kernels for 16%

profile of v1, /device:TPU:113, one launch (start us, length us, event | category | flops | bytes accessed | tf_op | source)
XLA Modules:
  0.0 207.5 jit_solution(12596587743427762759)
XLA Ops:
  6.5 0.0 all-gather.2.cloned.1.call-start
  6.5 1.4 pad_maximum_fusion
  7.9 0.0 all-gather.2.cloned.1.call-update
  8.0 0.8 copy.15
  8.7 0.1 reshape.125
  8.8 0.7 convert_reduce_fusion.1
  9.6 0.1 select_reduce_fusion.1
  9.7 0.1 select_reduce_fusion
  9.8 0.1 all_to_all.12
  9.9 0.1 copy.16
  10.0 10.6 %all_to_all.19 = s32[2,32,1]{0,2,1:T(1,128)S(1)} all-to-all(s32[2,32,1]{0,2,1:T(1,128)S(1)} %copy.16), channel_id=1, replica_groups=mesh['dp'=4,'db'=32] {'db'}, dimensions={1} | all-to-all | bytes 512 | tf_op jit(solution)/shard_map/all_to_all | solution.py:260
  20.6 1.9 slice_reduce_fusion
  22.5 5.8 %shard_map.83 = bf16[32,64,1024]{2,1,0:T(8,128)(2,1)} custom-call(s32[32]{0:T(128)} %get-tuple-element.6.rows_ref, bf16[64,64,1024]{2,1,0:T(8,128)(2,1)} %table_ref.3), custom_call_target="tpu_custom_call" | custom-call | bytes 8388608 | tf_op jit(solution)/shard_map/pallas_call | solution.py:37
  28.3 8.9 %all-to-all-start.1 = ((bf16[32,64,1024]{2,1,0:T(8,128)(2,1)}), bf16[32,64,1024]{2,1,0:T(8,128)(2,1)}, u32[]{:S(2)}, u32[]{:S(2)}) async-start(bf16[32,64,1024]{2,1,0:T(8,128)(2,1)} %shard_map.83), calls=%async_computation.1 | async-start | bytes 8388608 | tf_op jit(solution)/shard_map/all_to_all | solution.py:262
  37.2 7.7 %shard_map.85 = bf16[32,64,1024]{2,1,0:T(8,128)(2,1)} custom-call(s32[32]{0:T(128)} %get-tuple-element.5.rows_ref, bf16[64,64,1024]{2,1,0:T(8,128)(2,1)} %table_ref.3), custom_call_target="tpu_custom_call" | custom-call | bytes 8388608 | tf_op jit(solution)/shard_map/pallas_call | solution.py:37
  44.9 42.6 %all-to-all-done.1 = bf16[32,64,1024]{2,1,0:T(8,128)(2,1)} async-done(((bf16[32,64,1024]{2,1,0:T(8,128)(2,1)}), bf16[32,64,1024]{2,1,0:T(8,128)(2,1)}, u32[]{:S(2)}, u32[]{:S(2)}) %all-to-all-start.1) | async-done | bytes 4194336 | tf_op jit(solution)/shard_map/all_to_all | solution.py:262
  87.5 10.5 %all-to-all-start.2 = ((bf16[32,64,1024]{2,1,0:T(8,128)(2,1)}), bf16[32,64,1024]{2,1,0:T(8,128)(2,1)}, u32[]{:S(2)}, u32[]{:S(2)}) async-start(bf16[32,64,1024]{2,1,0:T(8,128)(2,1)} %shard_map.85), calls=%async_computation.2 | async-start | bytes 8388608 | tf_op jit(solution)/shard_map/all_to_all | solution.py:265
  98.1 0.1 select_reduce_fusion.2
  98.2 0.7 pad_add_fusion.meta_ref
  98.9 52.7 %all-gather.2.cloned.1.call-done.w_ref.w_key_ref.w_value_ref.w_out_ref = bf16[1024,4096]{1,0:T(8,128)(2,1)} async-done(((bf16[8,4096]{1,0:T(8,128)(2,1)}), bf16[1024,4096]{1,0:T(8,128)(2,1)}) %all-gather.2.cloned.1.call-update) | async-done | bytes 8388624 | tf_op jit(solution)/shard_map/all_gather | solution.py:246
  151.6 6.3 %shard_map.82.queries_ref = bf16[1024,1024]{1,0:T(8,128)(2,1)} custom-call(bf16[1024,1024]{1,0:T(8,128)(2,1)} %bitcast.6, f32[1,1024]{1,0:T(1,128)} %bitcast.8, bf16[1024,4096]{1,0:T(8,128)(2,1)} %all-gather.2.cloned.1.call-done.w_ref.w_key_ref.w_value_ref.w_out_ref), custom_call_target="tpu_custom_call" | custom-call | flops 2147483648 | bytes 6291456 | tf_op jit(solution)/shard_map/pallas_call | solution.py:66
  157.9 0.0 copy-start
  157.9 14.2 %shard_map.84 = bf16[2048,2048]{1,0:T(8,128)(2,1)} custom-call(bf16[2048,1024]{1,0:T(8,128)(2,1)} %bitcast.3.blocks_ref, bf16[1024,4096]{1,0:T(8,128)(2,1)} %all-gather.2.cloned.1.call-done.w_ref.w_key_ref.w_value_ref.w_out_ref, bf16[1024,4096]{1,0:T(8,128)(2,1)} %all-gather.2.cloned.1.call-done.w_ref.w_key_ref.w_value_ref.w_out_ref), custom_call_target="tpu_custom_call" | custom-call | flops 8589934592 | bytes 16777216 | tf_op jit(solution)/shard_map/pallas_call | solution.py:95
  172.1 0.0 all-to-all-done.2.second_ref
  172.1 0.0 copy-done
  172.1 0.0 copy-start.1
  172.1 1.6 copy-done.1
  173.7 26.9 %shard_map.86 = bf16[1024,1024]{1,0:T(8,128)(2,1)} custom-call(s32[65]{0:T(128)S(1)} %pad_add_fusion.meta_ref, bf16[1024,1024]{1,0:T(8,128)(2,1)S(1)} %bitcast.7, bf16[1024,1024]{1,0:T(8,128)(2,1)S(1)} %copy-done.1, bf16[1024,4096]{1,0:T(8,128)(2,1)} %all-gather.2.cloned.1.call-done.w_ref.w_key_ref.w_value_ref.w_out_ref, ...), custom_call_target="tpu_custom_call" | custom-call | flops 16106127360 | bytes 25165824 | tf_op jit(solution)/shard_map/pallas_call | solution.py:210
  (5 shorter events, 0.0 us)
Async XLA Ops:
  6.5 145.1 %all-gather.2.cloned.1.call-start = ((), (), s32[]{:S(2)}) async-start(), calls=%async_computation.3 | async-start | bytes 8454144 | tf_op jit(solution)/shard_map/all_gather | solution.py:246
  28.3 59.3 %all-to-all-start.1 = ((bf16[32,64,1024]{2,1,0:T(8,128)(2,1)}), bf16[32,64,1024]{2,1,0:T(8,128)(2,1)}, u32[]{:S(2)}, u32[]{:S(2)}) async-start(bf16[32,64,1024]{2,1,0:T(8,128)(2,1)} %shard_map.83), calls=%async_computation.1 | async-start | bytes 8388608 | tf_op jit(solution)/shard_map/all_to_all | solution.py:262
  87.5 84.6 %all-to-all-start.2 = ((bf16[32,64,1024]{2,1,0:T(8,128)(2,1)}), bf16[32,64,1024]{2,1,0:T(8,128)(2,1)}, u32[]{:S(2)}, u32[]{:S(2)}) async-start(bf16[32,64,1024]{2,1,0:T(8,128)(2,1)} %shard_map.85), calls=%async_computation.2 | async-start | bytes 8388608 | tf_op jit(solution)/shard_map/all_to_all | solution.py:265
  157.9 14.2 %copy-start = (bf16[16,64,1024]{2,1,0:T(8,128)(2,1)S(1)}, bf16[16,64,1024]{2,1,0:T(8,128)(2,1)}, u32[]{:S(2)}) copy-start(bf16[16,64,1024]{2,1,0:T(8,128)(2,1)} %param.8) | copy-start | bytes 6291460
  172.1 1.6 copy-start.1
Sparse Core Ops, SparseCore 0:
  10.3 141.2 all-gather.1
